TPU v7x, 32 devices: a whole 2x2x4 slice. The times are simulated.
32 devices in a mesh: lat: 8 (over y, x, core), lon: 4 (over z).
Axes of the slice: x: 2, y: 2, z: 4, core: 2. Of those that a mesh axis runs over, the one named last changes fastest.
Arguments:
- fields: bfloat16 [4, 64, 256, 640], P(None, 'lat', 'lon'), may hold values from -6 to 6
- kernel: float32 [64, 9, 3, 256], P('lat'), may hold values from -0.125 to 0.125
- theta: float32 [3, 640], P(None, 'lon'), may hold values from -4 to 4
- row_start: int32 [64], P('lat'), may hold values from 0 to 59, as said below
- row_count: int32 [64], P('lat'), may hold values from 1 to 9
- norm_gain: float32 [640], replicated, may hold values from 0.1 to 1.9
- w_in: bfloat16 [640, 1280], replicated, may hold values from -0.25 to 0.25
- b_in: float32 [1280], replicated, may hold values from -3 to 3
- w_out: bfloat16 [1280, 640], replicated, may hold values from -0.15625 to 0.15625
Outputs:
- block_out: bfloat16 [4, 64, 256, 640], P(None, 'lat', 'lon')
Inputs may be any that keep to these rules, and one draw needn't show every extreme that they name: Output row i draws on rows row_start[i] to row_start[i] + row_count[i] - 1, all inside the grid and within 4 rows of i.
All inputs are finite; a program needn't handle non-finite values.
Results may differ from a plain program's by a relative error of at most 0.0085.
Values may be sent and summed in bfloat16 or wider, within the bound.
A program may use at most 192 MiB of HBM per device.

v0:
```python
import functools
import math

import jax
import jax.numpy as jnp
from jax import lax
from jax.experimental import pallas as pl
from jax.experimental.pallas import tpu as pltpu
from jax.sharding import PartitionSpec as P

REACH = 4
WINDOW = 2 * REACH + 1
LANES = 128
MESH = pl.DeviceIdType.MESH


def block_kernel(
    L, T, members, fields, theta, kern_hbm, starts_hbm, counts_hbm, gain_hbm, w_in_hbm, b_in_hbm, w_out_hbm, out,
    wide, base, taps, kern, starts, counts, gain, w_in, b_in, w_out, theta_buf, staged, got, held, res,
    send_sem, recv_sem, halo_send, halo_recv, th_send, th_recv, local_sem, back_send, back_recv, own_sem, out_sem,
):
    lat, lon = lax.axis_index("lat"), lax.axis_index("lon")
    up, down = lax.rem(lat + 1, T), lax.rem(lat + T - 1, T)
    ens, rows, cols, chans = held.shape
    circle = wide.shape[2]
    slots, basis = kern.shape[:2]

    bring = pltpu.make_async_copy(fields, held, local_sem.at[2])
    bring.start()
    pairs = ((kern_hbm, kern), (starts_hbm, starts), (counts_hbm, counts), (gain_hbm, gain),
             (w_in_hbm, w_in), (b_in_hbm, b_in), (w_out_hbm, w_out))
    loads = [pltpu.make_async_copy(a, b, local_sem.at[3 + n]) for n, (a, b) in enumerate(pairs)]
    for copy in loads:
        copy.start()
    barrier = pltpu.get_barrier_semaphore()
    for step in range(1, L):
        pl.semaphore_signal(barrier, inc=1, device_id={"lon": lax.rem(lon + step, L)}, device_id_type=MESH)
    for other in (up, down):
        pl.semaphore_signal(barrier, inc=1, device_id={"lat": other}, device_id_type=MESH)
    pl.semaphore_wait(barrier, L + 1)

    def lons(owner):
        return pl.ds(pl.multiple_of(owner * cols, cols), cols)

    chunks = [(0, REACH)] + ([(REACH, rows - REACH)] if rows > REACH else [])
    sends = []
    for c, (low, size) in enumerate(chunks):
        row = []
        for step in range(1, L):
            peer = lax.rem(lon + step, L)
            row.append(pltpu.make_async_remote_copy(
                src_ref=fields.at[pl.ds(peer * members, members), pl.ds(low, size)],
                dst_ref=wide.at[:, pl.ds(REACH + low, size), lons(lon), :],
                send_sem=send_sem.at[c, step], recv_sem=recv_sem.at[c, step],
                device_id={"lon": peer}, device_id_type=MESH))
            row[-1].start()
        sends.append(row)
    shared = []
    for step in range(1, L):
        shared.append(pltpu.make_async_remote_copy(
            src_ref=theta, dst_ref=theta_buf.at[lon],
            send_sem=th_send.at[step], recv_sem=th_recv.at[step],
            device_id={"lon": lax.rem(lon + step, L)}, device_id_type=MESH))
        shared[-1].start()
    mine = pltpu.make_async_copy(
        fields.at[pl.ds(lon * members, members)], wide.at[:, pl.ds(REACH, rows), lons(lon), :], local_sem.at[0])
    mine_theta = pltpu.make_async_copy(theta, theta_buf.at[lon], local_sem.at[1])
    mine.start()
    mine_theta.start()
    mine.wait()
    mine_theta.wait()

    def forward(side, step, owner):
        source, target, other = ((REACH, REACH + rows, down), (rows, 0, up))[side]
        copy = pltpu.make_async_remote_copy(
            src_ref=wide.at[:, pl.ds(source, REACH), lons(owner), :],
            dst_ref=wide.at[:, pl.ds(target, REACH), lons(owner), :],
            send_sem=halo_send.at[side, step], recv_sem=halo_recv.at[side, step],
            device_id={"lat": other}, device_id_type=MESH)
        copy.start()
        return copy

    lower, upper = [forward(0, 0, lon)], [forward(1, 0, lon)]

    place = lax.broadcasted_iota(jnp.int32, (circle, circle), 0) + lax.broadcasted_iota(
        jnp.int32, (circle, circle), 1)
    flip = jnp.where((place == 0) | (place == circle), 1.0, 0.0).astype(jnp.bfloat16)

    for copy in loads[:3]:
        copy.wait()
    profiles = kern[...].reshape(slots * basis * rows, circle).astype(jnp.bfloat16)
    taps[...] = jnp.dot(profiles, flip, preferred_element_type=jnp.float32)

    def build_row(i, carry):
        shift = starts[i] - (lat * rows + i - REACH)
        count = counts[i]
        for w in range(WINDOW):
            slot = w - shift
            live = jnp.where((slot >= 0) & (slot < count), 1.0, 0.0)
            slot = jnp.clip(slot, 0, slots - 1)
            for k in range(basis):
                line = taps[pl.ds((slot * basis + k) * rows + i, 1), :] * live
                turned = pltpu.roll(jnp.broadcast_to(line, (LANES, circle)), 0, 1, stride=1, stride_axis=0)
                base[i, pl.ds(k * LANES, LANES), pl.ds(w * circle, circle)] = turned.astype(jnp.bfloat16)
        return carry

    lax.fori_loop(0, rows, build_row, 0)

    owners = [lax.rem(lon + L - step, L) for step in range(L)]
    for step in range(1, L):
        sends[0][step - 1].wait_recv()
        lower.append(forward(0, step, owners[step]))
    for copy in shared:
        copy.wait_recv()
    scale = jnp.concatenate([theta_buf[owner] for owner in range(L)], axis=1)
    for step in range(1, L):
        for row in sends[1:]:
            row[step - 1].wait_recv()
        upper.append(forward(1, step, owners[step]))
    for copy in lower:
        copy.wait_recv()

    def back(slot, step, e):
        peer = lax.rem(lon + step, L)
        return pltpu.make_async_remote_copy(
            src_ref=staged.at[e, slot, lons(peer), :], dst_ref=got.at[slot, lon * members + e],
            send_sem=back_send.at[slot, step, e], recv_sem=back_recv.at[slot, step, e],
            device_id={"lon": peer}, device_id_type=MESH)

    def own(slot, e):
        return pltpu.make_async_copy(
            staged.at[e, slot, lons(lon), :], got.at[slot, lon * members + e], own_sem.at[slot, e])

    blocks = circle // LANES

    def send_part(slot, h):
        for step in range(1, L):
            peer = lax.rem(lon + step, L)

            @pl.when((peer * cols + cols - 1) // LANES == h)
            def _():
                for e in range(members):
                    back(slot, step, e).start()

        if h == blocks - 1:
            for e in range(members):
                own(slot, e).start()

    def conv_row(slot, carry):
        i = lax.rem(slot + REACH, rows)
        for e in range(members):
            for h in range(circle // LANES):
                cut = h * LANES
                pieces = []
                for w in range(WINDOW):
                    pieces.append(wide[e, i + w, pl.ds(cut, circle - cut), :])
                    if cut:
                        pieces.append(wide[e, i + w, pl.ds(0, cut), :])
                prod = jnp.dot(base[i], jnp.concatenate(pieces, axis=0), preferred_element_type=jnp.float32)
                total = prod[:LANES] * scale[0:1, :]
                for k in range(1, basis):
                    total = total + prod[k * LANES:(k + 1) * LANES] * scale[k:k + 1, :]
                staged[e, slot, pl.ds(cut, LANES), :] = total.astype(jnp.bfloat16)
                if e == members - 1 and h > 0:
                    send_part(slot, h - 1)
                if e == 0 and h == 0:
                    @pl.when(slot > 0)
                    def _():
                        send_part(slot - 1, blocks - 1)
        return carry

    first = max(rows - REACH, 0)
    lax.fori_loop(0, first, conv_row, 0)
    for copy in upper:
        copy.wait_recv()
    lax.fori_loop(first, rows, conv_row, 0)
    for row in sends:
        for copy in row:
            copy.wait_send()
    for copy in shared + lower + upper:
        copy.wait_send()
    bring.wait()
    for copy in loads[3:]:
        copy.wait()

    def mlp_row(slot, carry):
        i = lax.rem(slot + REACH, rows)
        for e in range(members):
            for step in range(1, L):
                back(slot, step, e).wait_recv()
            own(slot, e).wait()
        values = got[slot].reshape(ens * cols, chans).astype(jnp.float32)
        mean = jnp.mean(values, axis=-1, keepdims=True)
        diff = values - mean
        var = jnp.mean(diff * diff, axis=-1, keepdims=True)
        normed = (diff * lax.rsqrt(var + 1e-05) * gain[...][None, :]).astype(jnp.bfloat16)
        hidden = jnp.dot(normed, w_in[...], preferred_element_type=jnp.float32) + b_in[...][None, :]
        hidden = (0.5 * hidden * (1.0 + lax.erf(hidden * math.sqrt(0.5)))).astype(jnp.bfloat16)

        @pl.when(slot == 0)
        def _():
            send_part(rows - 1, blocks - 1)

        branch = jnp.dot(hidden, w_out[...], preferred_element_type=jnp.float32)
        start = held[:, i].reshape(ens * cols, chans).astype(jnp.float32)
        res[slot] = (start + branch).astype(jnp.bfloat16).reshape(ens, cols, chans)

        @pl.when(slot > 0)
        def _():
            before = slot - 1
            pltpu.make_async_copy(res.at[before], out.at[:, lax.rem(before + REACH, rows)], out_sem.at[before]).start()
        return carry

    lax.fori_loop(0, rows, mlp_row, 0)
    pltpu.make_async_copy(res.at[rows - 1], out.at[:, (rows - 1 + REACH) % rows], out_sem.at[rows - 1]).start()
    for slot in range(rows):
        for e in range(members):
            for step in range(1, L):
                back(slot, step, e).wait_send()
        pltpu.make_async_copy(res.at[slot], out.at[:, (slot + REACH) % rows], out_sem.at[slot]).wait()


def block(fields, theta, kern, starts, counts, gain, w_in, b_in, w_out, L, T):
    ens, rows, cols, chans = fields.shape
    members, circle = ens // L, cols * L
    basis = theta.shape[0]
    any_space = pl.BlockSpec(memory_space=pl.ANY)
    dma = pltpu.SemaphoreType.DMA
    bf16 = jnp.bfloat16
    return pl.pallas_call(
        functools.partial(block_kernel, L, T, members),
        out_shape=jax.ShapeDtypeStruct(fields.shape, bf16),
        in_specs=[pl.BlockSpec(memory_space=pltpu.HBM)] * 9,
        out_specs=any_space,
        scratch_shapes=[
            pltpu.VMEM((members, rows + 2 * REACH, circle, chans), bf16),
            pltpu.VMEM((rows, basis * LANES, WINDOW * circle), bf16),
            pltpu.VMEM((kern.shape[0] * basis * rows, circle), jnp.float32),
            pltpu.VMEM(kern.shape, jnp.float32),
            pltpu.SMEM(starts.shape, jnp.int32),
            pltpu.SMEM(counts.shape, jnp.int32),
            pltpu.VMEM(gain.shape, jnp.float32),
            pltpu.VMEM(w_in.shape, bf16),
            pltpu.VMEM(b_in.shape, jnp.float32),
            pltpu.VMEM(w_out.shape, bf16),
            pltpu.VMEM((L,) + theta.shape, jnp.float32),
            pltpu.VMEM((members, rows, circle, chans), bf16),
            pltpu.VMEM((rows, ens, cols, chans), bf16),
            pltpu.VMEM(fields.shape, bf16),
            pltpu.VMEM((rows, ens, cols, chans), bf16),
            dma((2, L)), dma((2, L)), dma((2, L)), dma((2, L)), dma((L,)), dma((L,)), dma((10,)),
            dma((rows, L, members)), dma((rows, L, members)), dma((rows, members)), dma((rows,)),
        ],
        compiler_params=pltpu.CompilerParams(
            collective_id=0, has_side_effects=True, vmem_limit_bytes=58 * 2**20),
        name="block",
    )(fields, theta, kern, starts, counts, gain, w_in, b_in, w_out)


def with_halo(value, sides, width):
    for axis, dim in sides:
        size, length = (lax.axis_size(axis), value.shape[dim])
        up = [(i, (i + 1) % size) for i in range(size - 1)]
        down = [(j, i) for i, j in up]
        last = lax.slice_in_dim(value, length - width, length, axis=dim)
        initial = lax.slice_in_dim(value, 0, width, axis=dim)
        before = lax.ppermute(last, axis, up)
        after = lax.ppermute(initial, axis, down)
        value = jnp.concatenate([before, value, after], axis=dim)
    return value


def circle_tables(length):
    bins = length // 2 + 1
    points = jnp.arange(length, dtype=jnp.int32)
    freqs = jnp.arange(bins, dtype=jnp.int32)
    phase = points[:, None] * freqs[None, :] % length
    angle = phase.astype(jnp.float32) * (2.0 * math.pi / length)
    cosine = jnp.cos(angle)
    sine = jnp.sin(angle)
    onward = jnp.concatenate([cosine, -sine], axis=1)
    weight = jnp.where((freqs == 0) | (freqs == length // 2), 1.0, 2.0).astype(jnp.float32)
    backward = (
        jnp.concatenate([(cosine * weight[None, :]).T, (-sine * weight[None, :]).T], axis=0)
        / length
    )
    return (onward, backward, bins)


def forward(field, onward, bins):
    upper = onward.astype(jnp.bfloat16)
    lower = (onward - upper.astype(jnp.float32)).astype(jnp.bfloat16)
    spectrum = jnp.einsum("ejlc,lg->ejgc", field, upper, preferred_element_type=jnp.float32)
    spectrum = spectrum + jnp.einsum(
        "ejlc,lg->ejgc", field, lower, preferred_element_type=jnp.float32
    )
    return (spectrum[:, :, :bins], spectrum[:, :, bins:])


def mix_basis(kern_part, theta):
    mixed = kern_part[:, :, 0, :, None] * theta[0][None, None, None, :]
    for basis in range(1, kern_part.shape[2]):
        mixed = mixed + kern_part[:, :, basis, :, None] * theta[basis][None, None, None, :]
    return mixed


def spectral_shards(fields, kernel, theta, row_start, row_count, norm_gain, w_in, b_in, w_out):
    local = lax.all_to_all(fields, "lon", split_axis=3, concat_axis=2, tiled=True)
    members, band, circle, chans = local.shape
    onward, backward, bins = circle_tables(circle)
    widened = with_halo(local, (("lat", 1),), REACH)
    spec_re, spec_im = forward(widened, onward, bins)
    kern_all = jnp.einsum("irkm,mg->irkg", kernel, onward, precision=lax.Precision.HIGHEST)
    mixed_re = mix_basis(kern_all[..., :bins], theta)
    mixed_im = mix_basis(kern_all[..., bins:], theta)
    first_row = lax.axis_index("lat") * band - REACH
    span_rows = band + 2 * REACH
    slot_ids = jnp.arange(WINDOW, dtype=jnp.int32)
    offsets = row_start - first_row
    live_slot = slot_ids[None, :] < row_count[:, None]
    total_re = jnp.zeros((members, band, bins, chans), jnp.float32)
    total_im = jnp.zeros((members, band, bins, chans), jnp.float32)
    for span in range(span_rows):
        select = (live_slot & (offsets[:, None] + slot_ids[None, :] == span)).astype(jnp.float32)
        coef_re = jnp.einsum("is,isfc->ifc", select, mixed_re, precision=lax.Precision.HIGHEST)
        coef_im = jnp.einsum("is,isfc->ifc", select, mixed_im, precision=lax.Precision.HIGHEST)
        row_re = spec_re[:, span][:, None]
        row_im = spec_im[:, span][:, None]
        total_re = total_re + coef_re * row_re - coef_im * row_im
        total_im = total_im + coef_re * row_im + coef_im * row_re
    joined = jnp.concatenate([total_re, total_im], axis=2)
    conv = jnp.einsum("eigc,gl->eilc", joined, backward, precision=lax.Precision.HIGHEST).astype(
        jnp.bfloat16
    )
    values = lax.all_to_all(conv, "lon", split_axis=2, concat_axis=3, tiled=True).astype(
        jnp.float32
    )
    mean = jnp.mean(values, axis=-1, keepdims=True)
    var = jnp.mean((values - mean) ** 2, axis=-1, keepdims=True)
    normed = ((values - mean) * lax.rsqrt(var + 1e-05) * norm_gain).astype(jnp.bfloat16)
    hidden = jax.nn.gelu(
        jnp.einsum("eblc,ch->eblh", normed, w_in, preferred_element_type=jnp.float32) + b_in,
        approximate=False,
    ).astype(jnp.bfloat16)
    branch = jnp.einsum("eblh,hc->eblc", hidden, w_out, preferred_element_type=jnp.float32)
    return (fields.astype(jnp.float32) + branch).astype(jnp.bfloat16)


def shards(L, T, fields, kernel, theta, row_start, row_count, norm_gain, w_in, b_in, w_out):
    if fields.shape[0] % L:
        return spectral_shards(
            fields, kernel, theta, row_start, row_count, norm_gain, w_in, b_in, w_out
        )
    kern = jnp.transpose(kernel, (1, 2, 0, 3))
    return block(fields, theta, kern, row_start, row_count, norm_gain, w_in, b_in, w_out, L, T)


def solution(mesh):
    placed = (
        P(None, "lat", "lon", None),
        P("lat", None, None, None),
        P(None, "lon"),
        P("lat"),
        P("lat"),
        P(),
        P(),
        P(),
        P(),
    )
    return jax.shard_map(
        functools.partial(shards, mesh.shape["lon"], mesh.shape["lat"]),
        mesh=mesh, in_specs=placed, out_specs=P(None, "lat", "lon", None), check_vma=False,
    )
```

profile of v0, /device:TPU:0, one launch (start us, length us, event | category | flops | bytes accessed | tf_op | source)
XLA Modules:
  0.0 130.3 jit_solution(1945967176947402506)
XLA Ops:
  0.0 126.9 %block.1 = bf16[4,8,64,640]{3,2,1,0:T(8,128)(2,1)} custom-call(bf16[4,8,64,640]{3,2,1,0:T(8,128)(2,1)} %fields.1, f32[3,160]{1,0:T(4,128)} %theta.1, f32[9,3,8,256]{3,2,1,0:T(8,128)} %bitcast.1, s32[8]{0:T(128)} %starts_hbm.1, s32[8]{0:T(128)} %counts_hbm.1, f32[640]{0:T(1024)} %gain_hbm.1, bf16[640,1280]{1,0:T(8,128)(2,1)} %w_in_hbm.1, f32[1280]{0:T(1024)} %b_in_hbm.1, ...), custom_call_target="tpu_custom_call" | custom-call | tf_op jit(solution)/shard_map/block/pallas_call | solution.py:230
  126.9 3.5 %copy.11 = bf16[4,8,64,640]{3,2,1,0:T(8,128)(2,1)} copy(bf16[4,8,64,640]{3,2,1,0:T(8,128)(2,1)} %block.1) | data formatting | bytes 5242880
where the time goes:
time: 131 us; the launch traced here: 130 us
  Pallas kernels  127 us (97%)
  local copies, waits for them, and re-layouts  3.47 us (3%)
    pallas_call x1, Pallas kernels, block(): pl.pallas_call(functools.partial(block_kernel, L, T, members), out_shape=...  127 us
    unnamed x1, local copies, waits for them, and re-layouts  3.47 us

commit v1 on v0

--- a/solution.py
+++ b/solution.py
@@ -16,21 +16,23 @@
 
 def block_kernel(
     L, T, members, fields, theta, kern_hbm, starts_hbm, counts_hbm, gain_hbm, w_in_hbm, b_in_hbm, w_out_hbm, out,
-    wide, base, taps, kern, starts, counts, gain, w_in, b_in, w_out, theta_buf, staged, got, held, res,
-    send_sem, recv_sem, halo_send, halo_recv, th_send, th_recv, local_sem, back_send, back_recv, own_sem, out_sem,
+    wide_a, wide_b, base, taps, kern, starts, counts, gain, w_in, b_in, w_out, theta_buf,
+    staged_a, staged_b, got_a, got_b, held,
+    send_sem, recv_sem, halo_send, halo_recv, th_send, th_recv, local_sem, a_send, a_recv, b_send, b_recv,
 ):
     lat, lon = lax.axis_index("lat"), lax.axis_index("lon")
     up, down = lax.rem(lat + 1, T), lax.rem(lat + T - 1, T)
+    has_up, has_down = lat < T - 1, lat > 0
     ens, rows, cols, chans = held.shape
-    circle = wide.shape[2]
+    circle = wide_a.shape[2]
     slots, basis = kern.shape[:2]
-
-    bring = pltpu.make_async_copy(fields, held, local_sem.at[2])
-    bring.start()
+    head = wide_a.shape[3]
+    blocks = circle // LANES
+
     pairs = ((kern_hbm, kern), (starts_hbm, starts), (counts_hbm, counts), (gain_hbm, gain),
-             (w_in_hbm, w_in), (b_in_hbm, b_in), (w_out_hbm, w_out))
-    loads = [pltpu.make_async_copy(a, b, local_sem.at[3 + n]) for n, (a, b) in enumerate(pairs)]
-    for copy in loads:
+             (w_in_hbm, w_in), (b_in_hbm, b_in), (w_out_hbm, w_out), (fields, held), (theta, theta_buf.at[lon]))
+    loads = [pltpu.make_async_copy(a, b, local_sem.at[n]) for n, (a, b) in enumerate(pairs)]
+    for copy in loads[:3]:
         copy.start()
     barrier = pltpu.get_barrier_semaphore()
     for step in range(1, L):
@@ -42,45 +44,70 @@
     def lons(owner):
         return pl.ds(pl.multiple_of(owner * cols, cols), cols)
 
-    chunks = [(0, REACH)] + ([(REACH, rows - REACH)] if rows > REACH else [])
+    def member(owner):
+        return pl.ds(owner * members, members)
+
+    shared = []
+    for step in range(1, L):
+        shared.append(pltpu.make_async_remote_copy(
+            src_ref=theta, dst_ref=theta_buf.at[lon],
+            send_sem=th_send.at[step], recv_sem=th_recv.at[step],
+            device_id={"lon": lax.rem(lon + step, L)}, device_id_type=MESH))
+        shared[-1].start()
+    parts = [(wide_a, pl.ds(0, head), 0, rows), (wide_b, pl.ds(head, chans - head), 0, REACH)]
+    if rows > REACH:
+        parts.append((wide_b, pl.ds(head, chans - head), REACH, rows - REACH))
     sends = []
-    for c, (low, size) in enumerate(chunks):
+    for c, (wide, chan, low, size) in enumerate(parts):
         row = []
         for step in range(1, L):
             peer = lax.rem(lon + step, L)
             row.append(pltpu.make_async_remote_copy(
-                src_ref=fields.at[pl.ds(peer * members, members), pl.ds(low, size)],
+                src_ref=fields.at[member(peer), pl.ds(low, size), :, chan],
                 dst_ref=wide.at[:, pl.ds(REACH + low, size), lons(lon), :],
                 send_sem=send_sem.at[c, step], recv_sem=recv_sem.at[c, step],
                 device_id={"lon": peer}, device_id_type=MESH))
             row[-1].start()
         sends.append(row)
-    shared = []
-    for step in range(1, L):
-        shared.append(pltpu.make_async_remote_copy(
-            src_ref=theta, dst_ref=theta_buf.at[lon],
-            send_sem=th_send.at[step], recv_sem=th_recv.at[step],
-            device_id={"lon": lax.rem(lon + step, L)}, device_id_type=MESH))
-        shared[-1].start()
-    mine = pltpu.make_async_copy(
-        fields.at[pl.ds(lon * members, members)], wide.at[:, pl.ds(REACH, rows), lons(lon), :], local_sem.at[0])
-    mine_theta = pltpu.make_async_copy(theta, theta_buf.at[lon], local_sem.at[1])
-    mine.start()
-    mine_theta.start()
-    mine.wait()
-    mine_theta.wait()
-
-    def forward(side, step, owner):
-        source, target, other = ((REACH, REACH + rows, down), (rows, 0, up))[side]
+    mine = [
+        pltpu.make_async_copy(
+            fields.at[member(lon), :, :, chan], wide.at[:, pl.ds(REACH, rows), lons(lon), :], local_sem.at[len(pairs) + n])
+        for n, (wide, chan, _, _) in enumerate(parts[:2])]
+    for copy in mine + loads[3:]:
+        copy.start()
+
+    def forward(side, part, step, owner):
+        wide, chan = parts[part][:2]
+        source, target, other, there = ((0, REACH + rows, down, has_down), (rows - REACH, 0, up, has_up))[side]
+        if step:
+            src = wide.at[:, pl.ds(REACH + source, REACH), lons(owner), :]
+        else:
+            src = fields.at[member(owner), pl.ds(source, REACH), :, chan]
         copy = pltpu.make_async_remote_copy(
-            src_ref=wide.at[:, pl.ds(source, REACH), lons(owner), :],
-            dst_ref=wide.at[:, pl.ds(target, REACH), lons(owner), :],
-            send_sem=halo_send.at[side, step], recv_sem=halo_recv.at[side, step],
+            src_ref=src, dst_ref=wide.at[:, pl.ds(target, REACH), lons(owner), :],
+            send_sem=halo_send.at[side, part, step], recv_sem=halo_recv.at[side, part, step],
             device_id={"lat": other}, device_id_type=MESH)
-        copy.start()
+        pl.when(there)(copy.start)
         return copy
 
-    lower, upper = [forward(0, 0, lon)], [forward(1, 0, lon)]
+    def arrived(side, copies):
+        @pl.when((has_up, has_down)[side])
+        def _():
+            for copy in copies:
+                copy.wait_recv()
+
+    owners = [lax.rem(lon + L - step, L) for step in range(L)]
+    halo = [[[forward(side, part, 0, lon)] for part in range(2)] for side in range(2)]
+
+    @pl.when(lat == 0)
+    def _():
+        for wide in (wide_a, wide_b):
+            wide[:, :REACH] = jnp.zeros_like(wide[:, :REACH])
+
+    @pl.when(lat == T - 1)
+    def _():
+        for wide in (wide_a, wide_b):
+            wide[:, REACH + rows:] = jnp.zeros_like(wide[:, REACH + rows:])
 
     place = lax.broadcasted_iota(jnp.int32, (circle, circle), 0) + lax.broadcasted_iota(
         jnp.int32, (circle, circle), 1)
@@ -106,32 +133,75 @@
 
     lax.fori_loop(0, rows, build_row, 0)
 
-    owners = [lax.rem(lon + L - step, L) for step in range(L)]
-    for step in range(1, L):
-        sends[0][step - 1].wait_recv()
-        lower.append(forward(0, step, owners[step]))
     for copy in shared:
         copy.wait_recv()
+    loads[8].wait()
     scale = jnp.concatenate([theta_buf[owner] for owner in range(L)], axis=1)
-    for step in range(1, L):
-        for row in sends[1:]:
+
+    def window(wide, e, i, h):
+        cut = h * LANES
+        pieces = []
+        for w in range(WINDOW):
+            pieces.append(wide[e, i + w, pl.ds(cut, circle - cut), :])
+            if cut:
+                pieces.append(wide[e, i + w, pl.ds(0, cut), :])
+        return jnp.concatenate(pieces, axis=0)
+
+    def mixed(prod, scale):
+        total = prod[:LANES] * scale[0:1, :]
+        for k in range(1, basis):
+            total = total + prod[k * LANES:(k + 1) * LANES] * scale[k:k + 1, :]
+        return total.astype(jnp.bfloat16)
+
+    def head_row(slot, carry):
+        i = lax.rem(slot + REACH, rows)
+        for e in range(members):
+            both = jnp.concatenate([window(wide_a, e, i, h) for h in range(blocks)], axis=1)
+            prod = jnp.dot(base[i], both, preferred_element_type=jnp.float32)
+            for h in range(blocks):
+                staged_a[e, slot, pl.ds(h * LANES, LANES), :] = mixed(
+                    prod[:, h * head:(h + 1) * head], scale[:, :head])
+            got_a[slot, lon * members + e] = staged_a[e, slot, lons(lon), :]
+        return carry
+
+    first = max(rows - REACH, 0)
+    for step in range(1, L):
+        sends[0][step - 1].wait_recv()
+        for side in range(2):
+            halo[side][0].append(forward(side, 0, step, owners[step]))
+    mine[0].wait()
+    arrived(0, halo[0][0])
+    lax.fori_loop(0, first, head_row, 0)
+    arrived(1, halo[1][0])
+    lax.fori_loop(first, rows, head_row, 0)
+
+    def back_head(step, e):
+        peer = lax.rem(lon + step, L)
+        return pltpu.make_async_remote_copy(
+            src_ref=staged_a.at[e, :, lons(peer), :], dst_ref=got_a.at[:, lon * members + e],
+            send_sem=a_send.at[step, e], recv_sem=a_recv.at[step, e],
+            device_id={"lon": peer}, device_id_type=MESH)
+
+    for step in range(1, L):
+        for e in range(members):
+            back_head(step, e).start()
+
+    for step in range(1, L):
+        sends[1][step - 1].wait_recv()
+        halo[0][1].append(forward(0, 1, step, owners[step]))
+    for step in range(1, L):
+        for row in sends[2:]:
             row[step - 1].wait_recv()
-        upper.append(forward(1, step, owners[step]))
-    for copy in lower:
-        copy.wait_recv()
+        halo[1][1].append(forward(1, 1, step, owners[step]))
+    mine[1].wait()
+    arrived(0, halo[0][1])
 
     def back(slot, step, e):
         peer = lax.rem(lon + step, L)
         return pltpu.make_async_remote_copy(
-            src_ref=staged.at[e, slot, lons(peer), :], dst_ref=got.at[slot, lon * members + e],
-            send_sem=back_send.at[slot, step, e], recv_sem=back_recv.at[slot, step, e],
+            src_ref=staged_b.at[e, slot, lons(peer), :], dst_ref=got_b.at[slot, lon * members + e],
+            send_sem=b_send.at[slot, step, e], recv_sem=b_recv.at[slot, step, e],
             device_id={"lon": peer}, device_id_type=MESH)
-
-    def own(slot, e):
-        return pltpu.make_async_copy(
-            staged.at[e, slot, lons(lon), :], got.at[slot, lon * members + e], own_sem.at[slot, e])
-
-    blocks = circle // LANES
 
     def send_part(slot, h):
         for step in range(1, L):
@@ -142,54 +212,38 @@
                 for e in range(members):
                     back(slot, step, e).start()
 
-        if h == blocks - 1:
-            for e in range(members):
-                own(slot, e).start()
-
     def conv_row(slot, carry):
         i = lax.rem(slot + REACH, rows)
         for e in range(members):
-            for h in range(circle // LANES):
-                cut = h * LANES
-                pieces = []
-                for w in range(WINDOW):
-                    pieces.append(wide[e, i + w, pl.ds(cut, circle - cut), :])
-                    if cut:
-                        pieces.append(wide[e, i + w, pl.ds(0, cut), :])
-                prod = jnp.dot(base[i], jnp.concatenate(pieces, axis=0), preferred_element_type=jnp.float32)
-                total = prod[:LANES] * scale[0:1, :]
-                for k in range(1, basis):
-                    total = total + prod[k * LANES:(k + 1) * LANES] * scale[k:k + 1, :]
-                staged[e, slot, pl.ds(cut, LANES), :] = total.astype(jnp.bfloat16)
+            for h in range(blocks):
+                prod = jnp.dot(base[i], window(wide_b, e, i, h), preferred_element_type=jnp.float32)
+                staged_b[e, slot, pl.ds(h * LANES, LANES), :] = mixed(prod, scale[:, head:])
                 if e == members - 1 and h > 0:
                     send_part(slot, h - 1)
                 if e == 0 and h == 0:
                     @pl.when(slot > 0)
                     def _():
                         send_part(slot - 1, blocks - 1)
+            got_b[slot, lon * members + e] = staged_b[e, slot, lons(lon), :]
         return carry
 
-    first = max(rows - REACH, 0)
     lax.fori_loop(0, first, conv_row, 0)
-    for copy in upper:
-        copy.wait_recv()
+    arrived(1, halo[1][1])
     lax.fori_loop(first, rows, conv_row, 0)
-    for row in sends:
-        for copy in row:
-            copy.wait_send()
-    for copy in shared + lower + upper:
-        copy.wait_send()
-    bring.wait()
-    for copy in loads[3:]:
+    for copy in loads[3:8]:
         copy.wait()
+    for step in range(1, L):
+        for e in range(members):
+            back_head(step, e).wait_recv()
 
     def mlp_row(slot, carry):
         i = lax.rem(slot + REACH, rows)
         for e in range(members):
             for step in range(1, L):
                 back(slot, step, e).wait_recv()
-            own(slot, e).wait()
-        values = got[slot].reshape(ens * cols, chans).astype(jnp.float32)
+        values = jnp.concatenate(
+            [got_a[slot].reshape(ens * cols, head), got_b[slot].reshape(ens * cols, chans - head)], axis=1)
+        values = values.astype(jnp.float32)
         mean = jnp.mean(values, axis=-1, keepdims=True)
         diff = values - mean
         var = jnp.mean(diff * diff, axis=-1, keepdims=True)
@@ -203,37 +257,44 @@
 
         branch = jnp.dot(hidden, w_out[...], preferred_element_type=jnp.float32)
         start = held[:, i].reshape(ens * cols, chans).astype(jnp.float32)
-        res[slot] = (start + branch).astype(jnp.bfloat16).reshape(ens, cols, chans)
-
-        @pl.when(slot > 0)
+        out[:, i] = (start + branch).astype(jnp.bfloat16).reshape(ens, cols, chans)
+        return carry
+
+    lax.fori_loop(0, rows, mlp_row, 0)
+    for row in sends:
+        for copy in row:
+            copy.wait_send()
+    for copy in shared:
+        copy.wait_send()
+    for side in range(2):
+        @pl.when((has_down, has_up)[side])
         def _():
-            before = slot - 1
-            pltpu.make_async_copy(res.at[before], out.at[:, lax.rem(before + REACH, rows)], out_sem.at[before]).start()
-        return carry
-
-    lax.fori_loop(0, rows, mlp_row, 0)
-    pltpu.make_async_copy(res.at[rows - 1], out.at[:, (rows - 1 + REACH) % rows], out_sem.at[rows - 1]).start()
-    for slot in range(rows):
-        for e in range(members):
-            for step in range(1, L):
+            for part in halo[side]:
+                for copy in part:
+                    copy.wait_send()
+    for step in range(1, L):
+        for e in range(members):
+            back_head(step, e).wait_send()
+            for slot in range(rows):
                 back(slot, step, e).wait_send()
-        pltpu.make_async_copy(res.at[slot], out.at[:, (slot + REACH) % rows], out_sem.at[slot]).wait()
 
 
 def block(fields, theta, kern, starts, counts, gain, w_in, b_in, w_out, L, T):
     ens, rows, cols, chans = fields.shape
     members, circle = ens // L, cols * L
     basis = theta.shape[0]
-    any_space = pl.BlockSpec(memory_space=pl.ANY)
+    head = LANES
+    tail = chans - head
     dma = pltpu.SemaphoreType.DMA
     bf16 = jnp.bfloat16
     return pl.pallas_call(
         functools.partial(block_kernel, L, T, members),
-        out_shape=jax.ShapeDtypeStruct(fields.shape, bf16),
+        out_shape=pltpu.VMEM(fields.shape, bf16),
         in_specs=[pl.BlockSpec(memory_space=pltpu.HBM)] * 9,
-        out_specs=any_space,
+        out_specs=pl.BlockSpec(memory_space=pltpu.VMEM),
         scratch_shapes=[
-            pltpu.VMEM((members, rows + 2 * REACH, circle, chans), bf16),
+            pltpu.VMEM((members, rows + 2 * REACH, circle, head), bf16),
+            pltpu.VMEM((members, rows + 2 * REACH, circle, tail), bf16),
             pltpu.VMEM((rows, basis * LANES, WINDOW * circle), bf16),
             pltpu.VMEM((kern.shape[0] * basis * rows, circle), jnp.float32),
             pltpu.VMEM(kern.shape, jnp.float32),
@@ -244,15 +305,16 @@
             pltpu.VMEM(b_in.shape, jnp.float32),
             pltpu.VMEM(w_out.shape, bf16),
             pltpu.VMEM((L,) + theta.shape, jnp.float32),
-            pltpu.VMEM((members, rows, circle, chans), bf16),
-            pltpu.VMEM((rows, ens, cols, chans), bf16),
+            pltpu.VMEM((members, rows, circle, head), bf16),
+            pltpu.VMEM((members, rows, circle, tail), bf16),
+            pltpu.VMEM((rows, ens, cols, head), bf16),
+            pltpu.VMEM((rows, ens, cols, tail), bf16),
             pltpu.VMEM(fields.shape, bf16),
-            pltpu.VMEM((rows, ens, cols, chans), bf16),
-            dma((2, L)), dma((2, L)), dma((2, L)), dma((2, L)), dma((L,)), dma((L,)), dma((10,)),
-            dma((rows, L, members)), dma((rows, L, members)), dma((rows, members)), dma((rows,)),
+            dma((3, L)), dma((3, L)), dma((2, 2, L)), dma((2, 2, L)), dma((L,)), dma((L,)), dma((11,)),
+            dma((L, members)), dma((L, members)), dma((rows, L, members)), dma((rows, L, members)),
         ],
         compiler_params=pltpu.CompilerParams(
-            collective_id=0, has_side_effects=True, vmem_limit_bytes=58 * 2**20),
+            collective_id=0, has_side_effects=True, vmem_limit_bytes=52 * 2**20),
         name="block",
     )(fields, theta, kern, starts, counts, gain, w_in, b_in, w_out)
 

time: 131 us -> 123 us (0.939)
  Pallas kernels: 127 us -> 122 us
  local copies, waits for them, and re-layouts: 3.47 us -> 1.49 us
    pallas_call x1, Pallas kernels: 127 us -> 122 us  [block(): pl.pallas_call(functools.partial(block_kernel, L, T, members), out_shape=...]
    unnamed x1, local copies, waits for them, and re-layouts: 3.47 us -> 1.49 us
where the time goes in v1:
time: 123 us
  Pallas kernels  122 us (99%)
  local copies, waits for them, and re-layouts  1.49 us (1%)
    pallas_call x1, Pallas kernels, block(): pl.pallas_call(functools.partial(block_kernel, L, T, members), out_shape=...  122 us

profile of v1, /device:TPU:0, one launch (start us, length us, event | category | flops | bytes accessed | tf_op | source)
XLA Modules:
  0.0 123.2 jit_solution(596891856074443107)
XLA Ops:
  0.0 121.7 %block.1 = bf16[4,8,64,640]{3,2,1,0:T(8,128)(2,1)S(1)} custom-call(bf16[4,8,64,640]{3,2,1,0:T(8,128)(2,1)} %fields.1, f32[3,160]{1,0:T(4,128)} %theta.1, f32[9,3,8,256]{3,2,1,0:T(8,128)} %bitcast.1, s32[8]{0:T(128)} %starts_hbm.1, s32[8]{0:T(128)} %counts_hbm.1, f32[640]{0:T(1024)} %gain_hbm.1, bf16[640,1280]{1,0:T(8,128)(2,1)} %w_in_hbm.1, f32[1280]{0:T(1024)} %b_in_hbm.1, ...), custom_call_target="tpu_custom_call" | custom-call | tf_op jit(solution)/shard_map/block/pallas_call | solution.py:290
  121.7 1.5 %copy.11 = bf16[4,8,64,640]{3,2,1,0:T(8,128)(2,1)} copy(bf16[4,8,64,640]{3,2,1,0:T(8,128)(2,1)S(1)} %block.1) | data formatting | bytes 5242880

commit v2 on v1

--- a/solution.py
+++ b/solution.py
@@ -18,7 +18,7 @@
     L, T, members, fields, theta, kern_hbm, starts_hbm, counts_hbm, gain_hbm, w_in_hbm, b_in_hbm, w_out_hbm, out,
     wide_a, wide_b, base, taps, kern, starts, counts, gain, w_in, b_in, w_out, theta_buf,
     staged_a, staged_b, got_a, got_b, held,
-    send_sem, recv_sem, halo_send, halo_recv, th_send, th_recv, local_sem, a_send, a_recv, b_send, b_recv,
+    send_sem, recv_sem, halo_send, halo_recv, th_sem, local_sem, back_send, a_recv, b_recv,
 ):
     lat, lon = lax.axis_index("lat"), lax.axis_index("lon")
     up, down = lax.rem(lat + 1, T), lax.rem(lat + T - 1, T)
@@ -47,13 +47,11 @@
     def member(owner):
         return pl.ds(owner * members, members)
 
-    shared = []
     for step in range(1, L):
-        shared.append(pltpu.make_async_remote_copy(
+        pltpu.make_async_remote_copy(
             src_ref=theta, dst_ref=theta_buf.at[lon],
-            send_sem=th_send.at[step], recv_sem=th_recv.at[step],
-            device_id={"lon": lax.rem(lon + step, L)}, device_id_type=MESH))
-        shared[-1].start()
+            send_sem=th_sem.at[0], recv_sem=th_sem.at[1],
+            device_id={"lon": lax.rem(lon + step, L)}, device_id_type=MESH).start()
     parts = [(wide_a, pl.ds(0, head), 0, rows), (wide_b, pl.ds(head, chans - head), 0, REACH)]
     if rows > REACH:
         parts.append((wide_b, pl.ds(head, chans - head), REACH, rows - REACH))
@@ -65,7 +63,7 @@
             row.append(pltpu.make_async_remote_copy(
                 src_ref=fields.at[member(peer), pl.ds(low, size), :, chan],
                 dst_ref=wide.at[:, pl.ds(REACH + low, size), lons(lon), :],
-                send_sem=send_sem.at[c, step], recv_sem=recv_sem.at[c, step],
+                send_sem=send_sem.at[0], recv_sem=recv_sem.at[c, step - 1],
                 device_id={"lon": peer}, device_id_type=MESH))
             row[-1].start()
         sends.append(row)
@@ -85,19 +83,23 @@
             src = fields.at[member(owner), pl.ds(source, REACH), :, chan]
         copy = pltpu.make_async_remote_copy(
             src_ref=src, dst_ref=wide.at[:, pl.ds(target, REACH), lons(owner), :],
-            send_sem=halo_send.at[side, part, step], recv_sem=halo_recv.at[side, part, step],
+            send_sem=halo_send.at[side, part], recv_sem=halo_recv.at[side, part],
             device_id={"lat": other}, device_id_type=MESH)
         pl.when(there)(copy.start)
-        return copy
-
-    def arrived(side, copies):
+
+    def take(ref, sem):
+        pltpu.make_async_copy(ref, ref, sem).wait()
+
+    def arrived(side, part):
         @pl.when((has_up, has_down)[side])
         def _():
-            for copy in copies:
-                copy.wait_recv()
+            target = (REACH + rows, 0)[side]
+            take(parts[part][0].at[:, pl.ds(target, REACH)], halo_recv.at[side, part])
 
     owners = [lax.rem(lon + L - step, L) for step in range(L)]
-    halo = [[[forward(side, part, 0, lon)] for part in range(2)] for side in range(2)]
+    for side in range(2):
+        for part in range(2):
+            forward(side, part, 0, lon)
 
     @pl.when(lat == 0)
     def _():
@@ -133,8 +135,7 @@
 
     lax.fori_loop(0, rows, build_row, 0)
 
-    for copy in shared:
-        copy.wait_recv()
+    take(theta_buf.at[pl.ds(0, L - 1)], th_sem.at[1])
     loads[8].wait()
     scale = jnp.concatenate([theta_buf[owner] for owner in range(L)], axis=1)
 
@@ -153,6 +154,11 @@
             total = total + prod[k * LANES:(k + 1) * LANES] * scale[k:k + 1, :]
         return total.astype(jnp.bfloat16)
 
+    latest = jnp.where(lon < L // 2, L // 2, L // 2 - 1)
+
+    def place_of(source, target):
+        return lax.rem(source + L - (L // 2 if target < L // 2 else L // 2 - 1), L)
+
     def head_row(slot, carry):
         i = lax.rem(slot + REACH, rows)
         for e in range(members):
@@ -161,56 +167,61 @@
             for h in range(blocks):
                 staged_a[e, slot, pl.ds(h * LANES, LANES), :] = mixed(
                     prod[:, h * head:(h + 1) * head], scale[:, :head])
-            got_a[slot, lon * members + e] = staged_a[e, slot, lons(lon), :]
+            got_a[slot, lax.rem(lon + L - latest, L) * members + e] = staged_a[e, slot, lons(lon), :]
         return carry
 
     first = max(rows - REACH, 0)
     for step in range(1, L):
         sends[0][step - 1].wait_recv()
         for side in range(2):
-            halo[side][0].append(forward(side, 0, step, owners[step]))
+            forward(side, 0, step, owners[step])
     mine[0].wait()
-    arrived(0, halo[0][0])
+    arrived(0, 0)
     lax.fori_loop(0, first, head_row, 0)
-    arrived(1, halo[1][0])
+    arrived(1, 0)
     lax.fori_loop(first, rows, head_row, 0)
 
-    def back_head(step, e):
-        peer = lax.rem(lon + step, L)
+    def back_head(target, e):
         return pltpu.make_async_remote_copy(
-            src_ref=staged_a.at[e, :, lons(peer), :], dst_ref=got_a.at[:, lon * members + e],
-            send_sem=a_send.at[step, e], recv_sem=a_recv.at[step, e],
-            device_id={"lon": peer}, device_id_type=MESH)
-
-    for step in range(1, L):
-        for e in range(members):
-            back_head(step, e).start()
+            src_ref=staged_a.at[e, :, lons(target), :], dst_ref=got_a.at[:, place_of(lon, target) * members + e],
+            send_sem=back_send.at[0], recv_sem=a_recv.at[0],
+            device_id={"lon": target}, device_id_type=MESH)
+
+    outward = sorted(range(L), key=lambda p: min(p, L - 1 - p))
+    for target in outward:
+        @pl.when(lon != target)
+        def _():
+            for e in range(members):
+                back_head(target, e).start()
 
     for step in range(1, L):
         sends[1][step - 1].wait_recv()
-        halo[0][1].append(forward(0, 1, step, owners[step]))
+        forward(0, 1, step, owners[step])
     for step in range(1, L):
         for row in sends[2:]:
             row[step - 1].wait_recv()
-        halo[1][1].append(forward(1, 1, step, owners[step]))
+        forward(1, 1, step, owners[step])
     mine[1].wait()
-    arrived(0, halo[0][1])
-
-    def back(slot, step, e):
-        peer = lax.rem(lon + step, L)
+    arrived(0, 1)
+
+    def back(slot, target, e, late):
         return pltpu.make_async_remote_copy(
-            src_ref=staged_b.at[e, slot, lons(peer), :], dst_ref=got_b.at[slot, lon * members + e],
-            send_sem=b_send.at[slot, step, e], recv_sem=b_recv.at[slot, step, e],
-            device_id={"lon": peer}, device_id_type=MESH)
-
-    def send_part(slot, h):
-        for step in range(1, L):
-            peer = lax.rem(lon + step, L)
-
-            @pl.when((peer * cols + cols - 1) // LANES == h)
+            src_ref=staged_b.at[e, slot, lons(target), :], dst_ref=got_b.at[slot, place_of(lon, target) * members + e],
+            send_sem=back_send.at[0], recv_sem=b_recv.at[slot, 0 if late else 1],
+            device_id={"lon": target}, device_id_type=MESH)
+
+    def send_one(slot, target):
+        last = L // 2 if target < L // 2 else L // 2 - 1
+        for late in (False, True):
+            @pl.when((lon == last) if late else (lon != target) & (lon != last))
             def _():
                 for e in range(members):
-                    back(slot, step, e).start()
+                    back(slot, target, e, late).start()
+
+    def send_part(slot, h):
+        for target in outward:
+            if (target * cols + cols - 1) // LANES == h:
+                send_one(slot, target)
 
     def conv_row(slot, carry):
         i = lax.rem(slot + REACH, rows)
@@ -224,25 +235,24 @@
                     @pl.when(slot > 0)
                     def _():
                         send_part(slot - 1, blocks - 1)
-            got_b[slot, lon * members + e] = staged_b[e, slot, lons(lon), :]
+            got_b[slot, lax.rem(lon + L - latest, L) * members + e] = staged_b[e, slot, lons(lon), :]
         return carry
 
     lax.fori_loop(0, first, conv_row, 0)
-    arrived(1, halo[1][1])
+    arrived(1, 1)
     lax.fori_loop(first, rows, conv_row, 0)
     for copy in loads[3:8]:
         copy.wait()
-    for step in range(1, L):
-        for e in range(members):
-            back_head(step, e).wait_recv()
-
-    def mlp_row(slot, carry):
+    take(got_a.at[:, pl.ds(0, (L - 1) * members)], a_recv.at[0])
+
+    def mlp_part(slot, low, high):
         i = lax.rem(slot + REACH, rows)
-        for e in range(members):
-            for step in range(1, L):
-                back(slot, step, e).wait_recv()
+        fresh = (high - low - min(low, 1)) * members
+        take(got_b.at[slot, pl.ds(0, fresh)], b_recv.at[slot, min(low, 1)])
+        count = (high - low) * members
+        here = pl.ds(low * members, count)
         values = jnp.concatenate(
-            [got_a[slot].reshape(ens * cols, head), got_b[slot].reshape(ens * cols, chans - head)], axis=1)
+            [got_a[slot, here].reshape(count * cols, head), got_b[slot, here].reshape(count * cols, chans - head)], axis=1)
         values = values.astype(jnp.float32)
         mean = jnp.mean(values, axis=-1, keepdims=True)
         diff = values - mean
@@ -250,33 +260,34 @@
         normed = (diff * lax.rsqrt(var + 1e-05) * gain[...][None, :]).astype(jnp.bfloat16)
         hidden = jnp.dot(normed, w_in[...], preferred_element_type=jnp.float32) + b_in[...][None, :]
         hidden = (0.5 * hidden * (1.0 + lax.erf(hidden * math.sqrt(0.5)))).astype(jnp.bfloat16)
+        branch = jnp.dot(hidden, w_out[...], preferred_element_type=jnp.float32).reshape(high - low, members, cols, chans)
+        for g in range(low, high):
+            owned = pl.ds(lax.rem(latest + g, L) * members, members)
+            out[owned, i] = (held[owned, i].astype(jnp.float32) + branch[g - low]).astype(jnp.bfloat16)
+
+    def early_row(slot, carry):
+        mlp_part(slot, 1, L)
 
         @pl.when(slot == 0)
         def _():
             send_part(rows - 1, blocks - 1)
 
-        branch = jnp.dot(hidden, w_out[...], preferred_element_type=jnp.float32)
-        start = held[:, i].reshape(ens * cols, chans).astype(jnp.float32)
-        out[:, i] = (start + branch).astype(jnp.bfloat16).reshape(ens, cols, chans)
         return carry
 
-    lax.fori_loop(0, rows, mlp_row, 0)
-    for row in sends:
-        for copy in row:
-            copy.wait_send()
-    for copy in shared:
-        copy.wait_send()
+    def late_row(slot, carry):
+        mlp_part(slot, 0, 1)
+        return carry
+
+    lax.fori_loop(0, rows, early_row, 0)
+    take(held.at[pl.ds(0, (L - 1) * members)], send_sem.at[0])
+    take(theta_buf.at[pl.ds(0, L - 1)], th_sem.at[0])
     for side in range(2):
         @pl.when((has_down, has_up)[side])
         def _():
-            for part in halo[side]:
-                for copy in part:
-                    copy.wait_send()
-    for step in range(1, L):
-        for e in range(members):
-            back_head(step, e).wait_send()
-            for slot in range(rows):
-                back(slot, step, e).wait_send()
+            for part in range(2):
+                take(parts[part][0].at[:, pl.ds(0, REACH)], halo_send.at[side, part])
+    lax.fori_loop(0, rows, late_row, 0)
+    take(held.at[pl.ds(0, (L - 1) * members)], back_send.at[0])
 
 
 def block(fields, theta, kern, starts, counts, gain, w_in, b_in, w_out, L, T):
@@ -310,8 +321,7 @@
             pltpu.VMEM((rows, ens, cols, head), bf16),
             pltpu.VMEM((rows, ens, cols, tail), bf16),
             pltpu.VMEM(fields.shape, bf16),
-            dma((3, L)), dma((3, L)), dma((2, 2, L)), dma((2, 2, L)), dma((L,)), dma((L,)), dma((11,)),
-            dma((L, members)), dma((L, members)), dma((rows, L, members)), dma((rows, L, members)),
+            dma((1,)), dma((3, L - 1)), dma((2, 2)), dma((2, 2)), dma((2,)), dma((11,)), dma((1,)), dma((1,)), dma((rows, 2)),
         ],
         compiler_params=pltpu.CompilerParams(
             collective_id=0, has_side_effects=True, vmem_limit_bytes=52 * 2**20),

time: 123 us -> 122 us (level)
  Pallas kernels: 122 us -> 120 us
    pallas_call x1, Pallas kernels: 122 us -> 120 us  [block(): pl.pallas_call(functools.partial(block_kernel, L, T, members), out_shape=...]
where the time goes in v2:
time: 122 us
  Pallas kernels  120 us (98%)
  local copies, waits for them, and re-layouts  1.49 us (1%)
    pallas_call x1, Pallas kernels, block(): pl.pallas_call(functools.partial(block_kernel, L, T, members), out_shape=...  120 us

profile of v2, /device:TPU:0, one launch (start us, length us, event | category | flops | bytes accessed | tf_op | source)
XLA Modules:
  0.0 121.6 jit_solution(8990380254799808516)
XLA Ops:
  0.0 120.1 %block.1 = bf16[4,8,64,640]{3,2,1,0:T(8,128)(2,1)S(1)} custom-call(bf16[4,8,64,640]{3,2,1,0:T(8,128)(2,1)} %fields.1, f32[3,160]{1,0:T(4,128)} %theta.1, f32[9,3,8,256]{3,2,1,0:T(8,128)} %bitcast.1, s32[8]{0:T(128)} %starts_hbm.1, s32[8]{0:T(128)} %counts_hbm.1, f32[640]{0:T(1024)} %gain_hbm.1, bf16[640,1280]{1,0:T(8,128)(2,1)} %w_in_hbm.1, f32[1280]{0:T(1024)} %b_in_hbm.1, ...), custom_call_target="tpu_custom_call" | custom-call | tf_op jit(solution)/shard_map/block/pallas_call | solution.py:301
  120.1 1.5 %copy.11 = bf16[4,8,64,640]{3,2,1,0:T(8,128)(2,1)} copy(bf16[4,8,64,640]{3,2,1,0:T(8,128)(2,1)S(1)} %block.1) | data formatting | bytes 5242880

commit v3 on v2

--- a/solution.py
+++ b/solution.py
@@ -11,6 +11,7 @@
 REACH = 4
 WINDOW = 2 * REACH + 1
 LANES = 128
+BEHIND = 2
 MESH = pl.DeviceIdType.MESH
 
 
@@ -18,7 +19,7 @@
     L, T, members, fields, theta, kern_hbm, starts_hbm, counts_hbm, gain_hbm, w_in_hbm, b_in_hbm, w_out_hbm, out,
     wide_a, wide_b, base, taps, kern, starts, counts, gain, w_in, b_in, w_out, theta_buf,
     staged_a, staged_b, got_a, got_b, held,
-    send_sem, recv_sem, halo_send, halo_recv, th_sem, local_sem, back_send, a_recv, b_recv,
+    far_sem, lat_sem, send_sem, recv_sem, halo_send, halo_recv, th_sem, local_sem, back_send, a_recv, b_recv,
 ):
     lat, lon = lax.axis_index("lat"), lax.axis_index("lon")
     up, down = lax.rem(lat + 1, T), lax.rem(lat + T - 1, T)
@@ -35,11 +36,35 @@
     for copy in loads[:3]:
         copy.start()
     barrier = pltpu.get_barrier_semaphore()
-    for step in range(1, L):
-        pl.semaphore_signal(barrier, inc=1, device_id={"lon": lax.rem(lon + step, L)}, device_id_type=MESH)
-    for other in (up, down):
-        pl.semaphore_signal(barrier, inc=1, device_id={"lat": other}, device_id_type=MESH)
-    pl.semaphore_wait(barrier, L + 1)
+    half = L // 2
+    low = lon < half
+    inward, outward_by = jnp.where(low, lon + 1, lon - 1), jnp.where(low, lon - 1, lon + 1)
+    middle = (lon == half - 1) | (lon == half)
+    at_end = (lon == 0) | (lon == L - 1)
+    relayed = ((lon == 1) | (lon == L - 2)) if L > 3 else lon < 0
+    beside = ((down, has_down), (up, has_up))
+
+    def signal(sem, when, **device):
+        @pl.when(when)
+        def _():
+            pl.semaphore_signal(sem, inc=1, device_id=device, device_id_type=MESH)
+
+    signal(barrier, ~at_end, lon=outward_by)
+    signal(barrier, middle, lon=inward)
+    for other, there in beside:
+        signal(barrier, there & ~relayed, lat=other)
+    greeted = [jnp.where(there & ~relayed, 1, 0) for _, there in beside]
+    pl.semaphore_wait(barrier, 1 + greeted[0] + greeted[1])
+
+    def learn(side, when):
+        @pl.when(when)
+        def _():
+            pl.semaphore_wait(far_sem.at[side], 1)
+
+    def take(ref, sem):
+        pltpu.make_async_copy(ref, ref, sem).wait()
+
+    owners = [lax.rem(lon + L - step, L) for step in range(L)]
 
     def lons(owner):
         return pl.ds(pl.multiple_of(owner * cols, cols), cols)
@@ -47,26 +72,64 @@
     def member(owner):
         return pl.ds(owner * members, members)
 
-    for step in range(1, L):
-        pltpu.make_async_remote_copy(
-            src_ref=theta, dst_ref=theta_buf.at[lon],
-            send_sem=th_sem.at[0], recv_sem=th_sem.at[1],
-            device_id={"lon": lax.rem(lon + step, L)}, device_id_type=MESH).start()
     parts = [(wide_a, pl.ds(0, head), 0, rows), (wide_b, pl.ds(head, chans - head), 0, REACH)]
     if rows > REACH:
         parts.append((wide_b, pl.ds(head, chans - head), REACH, rows - REACH))
-    sends = []
-    for c, (wide, chan, low, size) in enumerate(parts):
-        row = []
-        for step in range(1, L):
-            peer = lax.rem(lon + step, L)
-            row.append(pltpu.make_async_remote_copy(
-                src_ref=fields.at[member(peer), pl.ds(low, size), :, chan],
-                dst_ref=wide.at[:, pl.ds(REACH + low, size), lons(lon), :],
-                send_sem=send_sem.at[0], recv_sem=recv_sem.at[c, step - 1],
-                device_id={"lon": peer}, device_id_type=MESH))
-            row[-1].start()
-        sends.append(row)
+    def send_theta(peer):
+        pltpu.make_async_remote_copy(
+            src_ref=theta, dst_ref=theta_buf.at[lon], send_sem=th_sem.at[0], recv_sem=th_sem.at[1],
+            device_id={"lon": peer}, device_id_type=MESH).start()
+
+    def outgoing(c, peer):
+        wide, chan, low, size = parts[c]
+        return pltpu.make_async_remote_copy(
+            src_ref=fields.at[member(peer), pl.ds(low, size), :, chan],
+            dst_ref=wide.at[:, pl.ds(REACH + low, size), lons(lon), :],
+            send_sem=send_sem.at[0], recv_sem=recv_sem.at[c, lax.rem(peer - lon + L, L) - 1],
+            device_id={"lon": peer}, device_id_type=MESH)
+
+    def incoming(c, step):
+        wide, chan, low, size = parts[c]
+        take(wide.at[:, pl.ds(REACH + low, size), lons(owners[step]), :], recv_sem.at[c, step - 1])
+
+    def both_ways(distance, act):
+        for peer, known in ((lon - distance, lon >= distance), (lon + distance, lon + distance < L)):
+            pl.when(known)(functools.partial(act, peer))
+
+    def begin(peer):
+        send_theta(peer)
+        outgoing(0, peer).start()
+
+    signal(far_sem.at[1], ~middle, lon=inward)
+    begin(inward)
+    for side, (other, there) in enumerate(beside):
+        signal(lat_sem.at[1 - side], there & at_end & (L > 3), lat=other)
+    inner_count = jnp.where(low, L - 1 - lon, lon)
+    outer_count = L - 1 - inner_count
+    for distance in range(1, L):
+        known = distance <= outer_count
+        learn(1, known)
+        signal(far_sem.at[1], known & ~middle, lon=inward)
+        if distance == 1:
+            signal(far_sem.at[0], known, lon=outward_by)
+            signal(far_sem.at[0], known & middle, lon=inward)
+        else:
+            signal(far_sem.at[0], known & middle, lon=inward)
+        pl.when(known)(functools.partial(begin, jnp.where(low, lon - distance, lon + distance)))
+        if distance > 1:
+            known = distance <= inner_count
+            learn(0, known)
+            signal(far_sem.at[0], known & ~at_end, lon=outward_by)
+            pl.when(known)(functools.partial(begin, jnp.where(low, lon + distance, lon - distance)))
+    for side, (other, there) in enumerate(beside):
+        @pl.when(there & (at_end | relayed) & (L > 3))
+        def _():
+            pl.semaphore_wait(lat_sem.at[side], 1)
+
+        signal(lat_sem.at[side], there & at_end & (L > 3), lon=inward)
+    for c in range(1, len(parts)):
+        for distance in range(1, L):
+            both_ways(distance, lambda peer: outgoing(c, peer).start())
     mine = [
         pltpu.make_async_copy(
             fields.at[member(lon), :, :, chan], wide.at[:, pl.ds(REACH, rows), lons(lon), :], local_sem.at[len(pairs) + n])
@@ -87,16 +150,12 @@
             device_id={"lat": other}, device_id_type=MESH)
         pl.when(there)(copy.start)
 
-    def take(ref, sem):
-        pltpu.make_async_copy(ref, ref, sem).wait()
-
     def arrived(side, part):
         @pl.when((has_up, has_down)[side])
         def _():
             target = (REACH + rows, 0)[side]
             take(parts[part][0].at[:, pl.ds(target, REACH)], halo_recv.at[side, part])
 
-    owners = [lax.rem(lon + L - step, L) for step in range(L)]
     for side in range(2):
         for part in range(2):
             forward(side, part, 0, lon)
@@ -172,7 +231,7 @@
 
     first = max(rows - REACH, 0)
     for step in range(1, L):
-        sends[0][step - 1].wait_recv()
+        incoming(0, step)
         for side in range(2):
             forward(side, 0, step, owners[step])
     mine[0].wait()
@@ -195,11 +254,11 @@
                 back_head(target, e).start()
 
     for step in range(1, L):
-        sends[1][step - 1].wait_recv()
+        incoming(1, step)
         forward(0, 1, step, owners[step])
     for step in range(1, L):
-        for row in sends[2:]:
-            row[step - 1].wait_recv()
+        for c in range(2, len(parts)):
+            incoming(c, step)
         forward(1, 1, step, owners[step])
     mine[1].wait()
     arrived(0, 1)
@@ -218,10 +277,17 @@
                 for e in range(members):
                     back(slot, target, e, late).start()
 
+    lag = [min(BEHIND, rows) if 0 < target < L // 2 else 0 for target in range(L)]
+
     def send_part(slot, h):
         for target in outward:
             if (target * cols + cols - 1) // LANES == h:
-                send_one(slot, target)
+                if lag[target]:
+                    @pl.when(slot >= lag[target])
+                    def _():
+                        send_one(slot - lag[target], target)
+                else:
+                    send_one(slot, target)
 
     def conv_row(slot, carry):
         i = lax.rem(slot + REACH, rows)
@@ -271,6 +337,9 @@
         @pl.when(slot == 0)
         def _():
             send_part(rows - 1, blocks - 1)
+            for target in range(L):
+                for behind in range(lag[target], 0, -1):
+                    send_one(rows - behind, target)
 
         return carry
 
@@ -321,7 +390,7 @@
             pltpu.VMEM((rows, ens, cols, head), bf16),
             pltpu.VMEM((rows, ens, cols, tail), bf16),
             pltpu.VMEM(fields.shape, bf16),
-            dma((1,)), dma((3, L - 1)), dma((2, 2)), dma((2, 2)), dma((2,)), dma((11,)), dma((1,)), dma((1,)), dma((rows, 2)),
+            pltpu.SemaphoreType.REGULAR((2,)), pltpu.SemaphoreType.REGULAR((2,)), dma((1,)), dma((3, L - 1)), dma((2, 2)), dma((2, 2)), dma((2,)), dma((11,)), dma((1,)), dma((1,)), dma((rows, 2)),
         ],
         compiler_params=pltpu.CompilerParams(
             collective_id=0, has_side_effects=True, vmem_limit_bytes=52 * 2**20),

time: 122 us -> 119 us (0.975); the launches traced: 122 us -> 117 us
  Pallas kernels: 120 us -> 115 us
    pallas_call x1, Pallas kernels: 120 us -> 115 us  [block(): pl.pallas_call(functools.partial(block_kernel, L, T, members), out_shape=...]
where the time goes in v3:
time: 119 us; the launch traced here: 117 us
  Pallas kernels  115 us (97%)
  local copies, waits for them, and re-layouts  1.49 us (1%)
    pallas_call x1, Pallas kernels, block(): pl.pallas_call(functools.partial(block_kernel, L, T, members), out_shape=...  115 us

profile of v3, /device:TPU:0, one launch (start us, length us, event | category | flops | bytes accessed | tf_op | source)
XLA Modules:
  0.0 116.9 jit_solution(203008958341981022)
XLA Ops:
  0.0 115.4 %block.1 = bf16[4,8,64,640]{3,2,1,0:T(8,128)(2,1)S(1)} custom-call(bf16[4,8,64,640]{3,2,1,0:T(8,128)(2,1)} %fields.1, f32[3,160]{1,0:T(4,128)} %theta.1, f32[9,3,8,256]{3,2,1,0:T(8,128)} %bitcast.1, s32[8]{0:T(128)} %starts_hbm.1, s32[8]{0:T(128)} %counts_hbm.1, f32[640]{0:T(1024)} %gain_hbm.1, bf16[640,1280]{1,0:T(8,128)(2,1)} %w_in_hbm.1, f32[1280]{0:T(1024)} %b_in_hbm.1, ...), custom_call_target="tpu_custom_call" | custom-call | tf_op jit(solution)/shard_map/block/pallas_call | solution.py:370
  115.4 1.5 %copy.11 = bf16[4,8,64,640]{3,2,1,0:T(8,128)(2,1)} copy(bf16[4,8,64,640]{3,2,1,0:T(8,128)(2,1)S(1)} %block.1) | data formatting | bytes 5242880

commit v4 on v3

--- a/solution.py
+++ b/solution.py
@@ -15,9 +15,48 @@
 MESH = pl.DeviceIdType.MESH
 
 
+def channel_mlp(first, rest, gain, w_in, b_in, w_out):
+    values = jnp.concatenate([first, rest], axis=1).astype(jnp.float32)
+    mean = jnp.mean(values, axis=-1, keepdims=True)
+    diff = values - mean
+    var = jnp.mean(diff * diff, axis=-1, keepdims=True)
+    normed = (diff * lax.rsqrt(var + 1e-05) * gain[...][None, :]).astype(jnp.bfloat16)
+    hidden = jnp.dot(normed, w_in[...], preferred_element_type=jnp.float32) + b_in[...][None, :]
+    hidden = (0.5 * hidden * (1.0 + lax.erf(hidden * math.sqrt(0.5)))).astype(jnp.bfloat16)
+    return jnp.dot(hidden, w_out[...], preferred_element_type=jnp.float32)
+
+
+def last_kernel(L, done, last_a, last_b, last_h, gain, w_in, b_in, w_out, out, piece, sem):
+    lon = lax.axis_index("lon")
+    ens, rows, cols, chans = out.shape
+    members, _, head = last_a.shape
+    latest = jnp.where(lon < L // 2, L // 2, L // 2 - 1)
+    final = (rows - 1 + REACH) % rows
+    others = [i for i in range(rows) if i != final]
+    early, later = others[:5], others[5:]
+    for i in early:
+        pltpu.make_async_copy(done.at[:, i], out.at[:, i], sem.at[0]).start()
+    branch = channel_mlp(
+        last_a[...].reshape(members * cols, head), last_b[...].reshape(members * cols, chans - head),
+        gain, w_in, b_in, w_out).reshape(members, cols, chans)
+    piece[...] = (last_h[...].astype(jnp.float32) + branch).astype(jnp.bfloat16)
+    copy = pltpu.make_async_copy(piece, out.at[pl.ds(latest * members, members), final], sem.at[1])
+    copy.start()
+    for i in later:
+        pltpu.make_async_copy(done.at[:, i], out.at[:, i], sem.at[0]).start()
+    for g in range(1, L):
+        owned = pl.ds(lax.rem(latest + g, L) * members, members)
+        pltpu.make_async_copy(done.at[owned, final], out.at[owned, final], sem.at[2]).start()
+    if rows > 1:
+        pltpu.make_async_copy(done.at[:, :rows - 1], out.at[:, :rows - 1], sem.at[0]).wait()
+    pltpu.make_async_copy(done.at[:ens - members, 0], out.at[:ens - members, 0], sem.at[2]).wait()
+    copy.wait()
+
+
 def block_kernel(
-    L, T, members, fields, theta, kern_hbm, starts_hbm, counts_hbm, gain_hbm, w_in_hbm, b_in_hbm, w_out_hbm, out,
-    wide_a, wide_b, base, taps, kern, starts, counts, gain, w_in, b_in, w_out, theta_buf,
+    L, T, members, fields, theta, kern_hbm, starts_hbm, counts_hbm, gain_hbm, w_in_hbm, b_in_hbm, w_out_hbm,
+    out, last_a, last_b, last_h, gain, w_in, b_in, w_out,
+    wide_a, wide_b, base, taps, kern, starts, counts, theta_buf,
     staged_a, staged_b, got_a, got_b, held,
     far_sem, lat_sem, send_sem, recv_sem, halo_send, halo_recv, th_sem, local_sem, back_send, a_recv, b_recv,
 ):
@@ -33,8 +72,6 @@
     pairs = ((kern_hbm, kern), (starts_hbm, starts), (counts_hbm, counts), (gain_hbm, gain),
              (w_in_hbm, w_in), (b_in_hbm, b_in), (w_out_hbm, w_out), (fields, held), (theta, theta_buf.at[lon]))
     loads = [pltpu.make_async_copy(a, b, local_sem.at[n]) for n, (a, b) in enumerate(pairs)]
-    for copy in loads[:3]:
-        copy.start()
     barrier = pltpu.get_barrier_semaphore()
     half = L // 2
     low = lon < half
@@ -97,11 +134,13 @@
             pl.when(known)(functools.partial(act, peer))
 
     def begin(peer):
+        outgoing(0, peer).start()
         send_theta(peer)
-        outgoing(0, peer).start()
-
+
+    begin(inward)
     signal(far_sem.at[1], ~middle, lon=inward)
-    begin(inward)
+    for copy in loads[:3]:
+        copy.start()
     for side, (other, there) in enumerate(beside):
         signal(lat_sem.at[1 - side], there & at_end & (L > 3), lat=other)
     inner_count = jnp.where(low, L - 1 - lon, lon)
@@ -132,8 +171,8 @@
             both_ways(distance, lambda peer: outgoing(c, peer).start())
     mine = [
         pltpu.make_async_copy(
-            fields.at[member(lon), :, :, chan], wide.at[:, pl.ds(REACH, rows), lons(lon), :], local_sem.at[len(pairs) + n])
-        for n, (wide, chan, _, _) in enumerate(parts[:2])]
+            fields.at[member(lon), :, :, chan], wide.at[:, pl.ds(REACH, rows), lons(lon), :], local_sem.at[len(pairs)])
+        for wide, chan, _, _ in parts[:2]]
     for copy in mine + loads[3:]:
         copy.start()
 
@@ -146,7 +185,7 @@
             src = fields.at[member(owner), pl.ds(source, REACH), :, chan]
         copy = pltpu.make_async_remote_copy(
             src_ref=src, dst_ref=wide.at[:, pl.ds(target, REACH), lons(owner), :],
-            send_sem=halo_send.at[side, part], recv_sem=halo_recv.at[side, part],
+            send_sem=halo_send.at[side], recv_sem=halo_recv.at[side, part],
             device_id={"lat": other}, device_id_type=MESH)
         pl.when(there)(copy.start)
 
@@ -234,7 +273,7 @@
         incoming(0, step)
         for side in range(2):
             forward(side, 0, step, owners[step])
-    mine[0].wait()
+    take(held.at[member(0)], local_sem.at[len(pairs)])
     arrived(0, 0)
     lax.fori_loop(0, first, head_row, 0)
     arrived(1, 0)
@@ -260,7 +299,6 @@
         for c in range(2, len(parts)):
             incoming(c, step)
         forward(1, 1, step, owners[step])
-    mine[1].wait()
     arrived(0, 1)
 
     def back(slot, target, e, late):
@@ -317,16 +355,9 @@
         take(got_b.at[slot, pl.ds(0, fresh)], b_recv.at[slot, min(low, 1)])
         count = (high - low) * members
         here = pl.ds(low * members, count)
-        values = jnp.concatenate(
-            [got_a[slot, here].reshape(count * cols, head), got_b[slot, here].reshape(count * cols, chans - head)], axis=1)
-        values = values.astype(jnp.float32)
-        mean = jnp.mean(values, axis=-1, keepdims=True)
-        diff = values - mean
-        var = jnp.mean(diff * diff, axis=-1, keepdims=True)
-        normed = (diff * lax.rsqrt(var + 1e-05) * gain[...][None, :]).astype(jnp.bfloat16)
-        hidden = jnp.dot(normed, w_in[...], preferred_element_type=jnp.float32) + b_in[...][None, :]
-        hidden = (0.5 * hidden * (1.0 + lax.erf(hidden * math.sqrt(0.5)))).astype(jnp.bfloat16)
-        branch = jnp.dot(hidden, w_out[...], preferred_element_type=jnp.float32).reshape(high - low, members, cols, chans)
+        branch = channel_mlp(
+            got_a[slot, here].reshape(count * cols, head), got_b[slot, here].reshape(count * cols, chans - head),
+            gain, w_in, b_in, w_out).reshape(high - low, members, cols, chans)
         for g in range(low, high):
             owned = pl.ds(lax.rem(latest + g, L) * members, members)
             out[owned, i] = (held[owned, i].astype(jnp.float32) + branch[g - low]).astype(jnp.bfloat16)
@@ -353,9 +384,13 @@
     for side in range(2):
         @pl.when((has_down, has_up)[side])
         def _():
-            for part in range(2):
-                take(parts[part][0].at[:, pl.ds(0, REACH)], halo_send.at[side, part])
-    lax.fori_loop(0, rows, late_row, 0)
+            take(held.at[:, pl.ds(0, REACH)], halo_send.at[side])
+    lax.fori_loop(0, rows - 1, late_row, 0)
+    final = (rows - 1 + REACH) % rows
+    last_h[...] = held[pl.ds(latest * members, members), final]
+    last_a[...] = got_a[rows - 1, pl.ds(0, members)]
+    take(got_b.at[rows - 1, pl.ds(0, members)], b_recv.at[rows - 1, 0])
+    last_b[...] = got_b[rows - 1, pl.ds(0, members)]
     take(held.at[pl.ds(0, (L - 1) * members)], back_send.at[0])
 
 
@@ -367,11 +402,16 @@
     tail = chans - head
     dma = pltpu.SemaphoreType.DMA
     bf16 = jnp.bfloat16
-    return pl.pallas_call(
+    kept = (
+        pltpu.VMEM(fields.shape, bf16), pltpu.VMEM((members, cols, head), bf16), pltpu.VMEM((members, cols, tail), bf16),
+        pltpu.VMEM((members, cols, chans), bf16), pltpu.VMEM(gain.shape, jnp.float32), pltpu.VMEM(w_in.shape, bf16),
+        pltpu.VMEM(b_in.shape, jnp.float32), pltpu.VMEM(w_out.shape, bf16))
+    in_vmem = pl.BlockSpec(memory_space=pltpu.VMEM)
+    parts = pl.pallas_call(
         functools.partial(block_kernel, L, T, members),
-        out_shape=pltpu.VMEM(fields.shape, bf16),
+        out_shape=kept,
         in_specs=[pl.BlockSpec(memory_space=pltpu.HBM)] * 9,
-        out_specs=pl.BlockSpec(memory_space=pltpu.VMEM),
+        out_specs=[in_vmem] * len(kept),
         scratch_shapes=[
             pltpu.VMEM((members, rows + 2 * REACH, circle, head), bf16),
             pltpu.VMEM((members, rows + 2 * REACH, circle, tail), bf16),
@@ -380,22 +420,28 @@
             pltpu.VMEM(kern.shape, jnp.float32),
             pltpu.SMEM(starts.shape, jnp.int32),
             pltpu.SMEM(counts.shape, jnp.int32),
-            pltpu.VMEM(gain.shape, jnp.float32),
-            pltpu.VMEM(w_in.shape, bf16),
-            pltpu.VMEM(b_in.shape, jnp.float32),
-            pltpu.VMEM(w_out.shape, bf16),
             pltpu.VMEM((L,) + theta.shape, jnp.float32),
             pltpu.VMEM((members, rows, circle, head), bf16),
             pltpu.VMEM((members, rows, circle, tail), bf16),
             pltpu.VMEM((rows, ens, cols, head), bf16),
             pltpu.VMEM((rows, ens, cols, tail), bf16),
             pltpu.VMEM(fields.shape, bf16),
-            pltpu.SemaphoreType.REGULAR((2,)), pltpu.SemaphoreType.REGULAR((2,)), dma((1,)), dma((3, L - 1)), dma((2, 2)), dma((2, 2)), dma((2,)), dma((11,)), dma((1,)), dma((1,)), dma((rows, 2)),
+            pltpu.SemaphoreType.REGULAR((2,)), pltpu.SemaphoreType.REGULAR((2,)), dma((1,)), dma((3, L - 1)), dma((2,)), dma((2, 2)), dma((2,)), dma((10,)), dma((1,)), dma((1,)), dma((rows, 2)),
         ],
         compiler_params=pltpu.CompilerParams(
-            collective_id=0, has_side_effects=True, vmem_limit_bytes=52 * 2**20),
+            collective_id=0, has_side_effects=True, vmem_limit_bytes=48 * 2**20),
         name="block",
-    )(fields, theta, kern, starts, counts, gain, w_in, b_in, w_out)
+    )(*(pltpu.with_memory_space_constraint(v, pltpu.HBM)
+        for v in (fields, theta, kern, starts, counts, gain, w_in, b_in, w_out)))
+    return pl.pallas_call(
+        functools.partial(last_kernel, L),
+        out_shape=jax.ShapeDtypeStruct(fields.shape, bf16),
+        in_specs=[in_vmem] * len(kept),
+        out_specs=pl.BlockSpec(memory_space=pltpu.HBM),
+        scratch_shapes=[pltpu.VMEM((members, cols, chans), bf16), dma((3,))],
+        compiler_params=pltpu.CompilerParams(vmem_limit_bytes=8 * 2**20),
+        name="last",
+    )(*parts)
 
 
 def with_halo(value, sides, width):
@@ -488,7 +534,7 @@
 
 
 def shards(L, T, fields, kernel, theta, row_start, row_count, norm_gain, w_in, b_in, w_out):
-    if fields.shape[0] % L:
+    if L == 1 or fields.shape[0] % L:
         return spectral_shards(
             fields, kernel, theta, row_start, row_count, norm_gain, w_in, b_in, w_out
         )

time: 119 us -> 118 us (level)
  local copies, waits for them, and re-layouts: 1.49 us -> 0 us
    pallas_call x0 -> x1, Pallas kernels: none -> 1.8 us  [block(): pl.pallas_call(functools.partial(last_kernel, L), out_shape=jax.ShapeDtyp...]
    unnamed x1 -> x0, local copies, waits for them, and re-layouts: 1.49 us -> none
where the time goes in v4:
time: 118 us; the launch traced here: 116 us
  Pallas kernels  116 us (98%)
    pallas_call x1, Pallas kernels, block(): pl.pallas_call(functools.partial(block_kernel, L, T, members), out_shape=...  114 us

profile of v4, /device:TPU:0, one launch (start us, length us, event | category | flops | bytes accessed | tf_op | source)
XLA Modules:
  0.0 116.3 jit_solution(3587913222946520941)
XLA Ops:
  0.0 114.5 %block.1 = (bf16[4,8,64,640]{3,2,1,0:T(8,128)(2,1)S(1)}, bf16[1,64,128]{2,1,0:T(8,128)(2,1)S(1)}, bf16[1,64,512]{2,1,0:T(8,128)(2,1)S(1)}, bf16[1,64,640]{2,1,0:...) custom-call(bf16[4,8,64,640]{3,2,1,0:T(8,128)(2,1)} %fields.1, ...), custom_call_target="tpu_custom_call" | custom-call | tf_op jit(solution)/shard_map/block/pallas_call | solution.py:410
  114.5 1.8 %last.1 = bf16[4,8,64,640]{3,2,1,0:T(8,128)(2,1)} custom-call(bf16[4,8,64,640]{3,2,1,0:T(8,128)(2,1)S(1)} %get-tuple-element.13.done, bf16[1,64,128]{2,1,0:T(8,128)(2,1)S(1)} %get-tuple-element.14.last_a, bf16[1,64,512]{2,1,0:T(8,128)(2,1)S(1)} %get-tuple-element.15.last_b, bf16[1,64,640]{2,1,0:T(8,128)(2,1)S(1)} %get-tuple-element.16.last_h, ...), custom_call_target="tpu_custom_call" | custom-call | tf_op jit(solution)/shard_map/last/pallas_call | solution.py:436

commit v5 on v4

--- a/solution.py
+++ b/solution.py
@@ -32,18 +32,18 @@
     members, _, head = last_a.shape
     latest = jnp.where(lon < L // 2, L // 2, L // 2 - 1)
     final = (rows - 1 + REACH) % rows
-    others = [i for i in range(rows) if i != final]
-    early, later = others[:5], others[5:]
-    for i in early:
-        pltpu.make_async_copy(done.at[:, i], out.at[:, i], sem.at[0]).start()
+    for e in range(ens):
+        pltpu.make_async_copy(done.at[e, final + 1:], out.at[e, final + 1:], sem.at[0]).start()
+        if e < ens // 2:
+            pltpu.make_async_copy(done.at[e, :final], out.at[e, :final], sem.at[0]).start()
     branch = channel_mlp(
         last_a[...].reshape(members * cols, head), last_b[...].reshape(members * cols, chans - head),
         gain, w_in, b_in, w_out).reshape(members, cols, chans)
     piece[...] = (last_h[...].astype(jnp.float32) + branch).astype(jnp.bfloat16)
     copy = pltpu.make_async_copy(piece, out.at[pl.ds(latest * members, members), final], sem.at[1])
     copy.start()
-    for i in later:
-        pltpu.make_async_copy(done.at[:, i], out.at[:, i], sem.at[0]).start()
+    for e in range(ens // 2, ens):
+        pltpu.make_async_copy(done.at[e, :final], out.at[e, :final], sem.at[0]).start()
     for g in range(1, L):
         owned = pl.ds(lax.rem(latest + g, L) * members, members)
         pltpu.make_async_copy(done.at[owned, final], out.at[owned, final], sem.at[2]).start()
@@ -286,15 +286,15 @@
             device_id={"lon": target}, device_id_type=MESH)
 
     outward = sorted(range(L), key=lambda p: min(p, L - 1 - p))
-    for target in outward:
-        @pl.when(lon != target)
-        def _():
-            for e in range(members):
-                back_head(target, e).start()
-
     for step in range(1, L):
         incoming(1, step)
         forward(0, 1, step, owners[step])
+        if step == 1:
+            for target in outward:
+                @pl.when(lon != target)
+                def _():
+                    for e in range(members):
+                        back_head(target, e).start()
     for step in range(1, L):
         for c in range(2, len(parts)):
             incoming(c, step)
@@ -352,7 +352,8 @@
     def mlp_part(slot, low, high):
         i = lax.rem(slot + REACH, rows)
         fresh = (high - low - min(low, 1)) * members
-        take(got_b.at[slot, pl.ds(0, fresh)], b_recv.at[slot, min(low, 1)])
+        if fresh:
+            take(got_b.at[slot, pl.ds(0, fresh)], b_recv.at[slot, min(low, 1)])
         count = (high - low) * members
         here = pl.ds(low * members, count)
         branch = channel_mlp(

time: 118 us -> 118 us (level)
  no operation moved by 1% of the time
where the time goes in v5:
time: 118 us; the launch traced here: 116 us
  Pallas kernels  116 us (98%)
    pallas_call x1, Pallas kernels, block(): pl.pallas_call(functools.partial(block_kernel, L, T, members), out_shape=...  114 us

profile of v5, /device:TPU:0, one launch (start us, length us, event | category | flops | bytes accessed | tf_op | source)
XLA Modules:
  0.0 116.3 jit_solution(16650633803882875545)
XLA Ops:
  0.0 114.5 %block.1 = (bf16[4,8,64,640]{3,2,1,0:T(8,128)(2,1)S(1)}, bf16[1,64,128]{2,1,0:T(8,128)(2,1)S(1)}, bf16[1,64,512]{2,1,0:T(8,128)(2,1)S(1)}, bf16[1,64,640]{2,1,0:...) custom-call(bf16[4,8,64,640]{3,2,1,0:T(8,128)(2,1)} %fields.1, ...), custom_call_target="tpu_custom_call" | custom-call | tf_op jit(solution)/shard_map/block/pallas_call | solution.py:411
  114.5 1.7 %last.1 = bf16[4,8,64,640]{3,2,1,0:T(8,128)(2,1)} custom-call(bf16[4,8,64,640]{3,2,1,0:T(8,128)(2,1)S(1)} %get-tuple-element.13.done, bf16[1,64,128]{2,1,0:T(8,128)(2,1)S(1)} %get-tuple-element.14.last_a, bf16[1,64,512]{2,1,0:T(8,128)(2,1)S(1)} %get-tuple-element.15.last_b, bf16[1,64,640]{2,1,0:T(8,128)(2,1)S(1)} %get-tuple-element.16.last_h, ...), custom_call_target="tpu_custom_call" | custom-call | tf_op jit(solution)/shard_map/last/pallas_call | solution.py:437

commit v6 on v5

--- a/solution.py
+++ b/solution.py
@@ -58,7 +58,7 @@
     out, last_a, last_b, last_h, gain, w_in, b_in, w_out,
     wide_a, wide_b, base, taps, kern, starts, counts, theta_buf,
     staged_a, staged_b, got_a, got_b, held,
-    far_sem, lat_sem, send_sem, recv_sem, halo_send, halo_recv, th_sem, local_sem, back_send, a_recv, b_recv,
+    far_sem, lat_sem, send_sem, recv_sem, halo_send, halo_recv, th_sem, local_sem, back_send, a_recv, early_recv, late_recv, first_recv,
 ):
     lat, lon = lax.axis_index("lat"), lax.axis_index("lon")
     up, down = lax.rem(lat + 1, T), lax.rem(lat + T - 1, T)
@@ -68,6 +68,8 @@
     slots, basis = kern.shape[:2]
     head = wide_a.shape[3]
     blocks = circle // LANES
+    pair = 2 - rows % 2
+    pooled = max(rows // 2 - 1, 0)
 
     pairs = ((kern_hbm, kern), (starts_hbm, starts), (counts_hbm, counts), (gain_hbm, gain),
              (w_in_hbm, w_in), (b_in_hbm, b_in), (w_out_hbm, w_out), (fields, held), (theta, theta_buf.at[lon]))
@@ -122,12 +124,12 @@
         return pltpu.make_async_remote_copy(
             src_ref=fields.at[member(peer), pl.ds(low, size), :, chan],
             dst_ref=wide.at[:, pl.ds(REACH + low, size), lons(lon), :],
-            send_sem=send_sem.at[0], recv_sem=recv_sem.at[c, lax.rem(peer - lon + L, L) - 1],
+            send_sem=send_sem.at[0], recv_sem=recv_sem.at[c - 1, lax.rem(peer - lon + L, L) - 1] if c else first_recv.at[0],
             device_id={"lon": peer}, device_id_type=MESH)
 
     def incoming(c, step):
         wide, chan, low, size = parts[c]
-        take(wide.at[:, pl.ds(REACH + low, size), lons(owners[step]), :], recv_sem.at[c, step - 1])
+        take(wide.at[:, pl.ds(REACH + low, size), lons(owners[step]), :], recv_sem.at[c - 1, step - 1])
 
     def both_ways(distance, act):
         for peer, known in ((lon - distance, lon >= distance), (lon + distance, lon + distance < L)):
@@ -269,8 +271,8 @@
         return carry
 
     first = max(rows - REACH, 0)
+    take(got_a.at[:, pl.ds(0, (L - 1) * members)], first_recv.at[0])
     for step in range(1, L):
-        incoming(0, step)
         for side in range(2):
             forward(side, 0, step, owners[step])
     take(held.at[member(0)], local_sem.at[len(pairs)])
@@ -304,7 +306,7 @@
     def back(slot, target, e, late):
         return pltpu.make_async_remote_copy(
             src_ref=staged_b.at[e, slot, lons(target), :], dst_ref=got_b.at[slot, place_of(lon, target) * members + e],
-            send_sem=back_send.at[0], recv_sem=b_recv.at[slot, 0 if late else 1],
+            send_sem=back_send.at[0], recv_sem=late_recv.at[jnp.maximum(slot - pooled, 0)] if late else early_recv.at[slot // pair],
             device_id={"lon": target}, device_id_type=MESH)
 
     def send_one(slot, target):
@@ -352,8 +354,14 @@
     def mlp_part(slot, low, high):
         i = lax.rem(slot + REACH, rows)
         fresh = (high - low - min(low, 1)) * members
-        if fresh:
-            take(got_b.at[slot, pl.ds(0, fresh)], b_recv.at[slot, min(low, 1)])
+        if fresh and low:
+            @pl.when(slot % pair == 0)
+            def _():
+                take(got_b.at[pl.ds(slot, pair), pl.ds(0, fresh)], early_recv.at[slot // pair])
+        elif fresh:
+            @pl.when(slot > pooled)
+            def _():
+                take(got_b.at[slot, pl.ds(0, fresh)], late_recv.at[slot - pooled])
         count = (high - low) * members
         here = pl.ds(low * members, count)
         branch = channel_mlp(
@@ -386,11 +394,12 @@
         @pl.when((has_down, has_up)[side])
         def _():
             take(held.at[:, pl.ds(0, REACH)], halo_send.at[side])
+    take(got_b.at[pl.ds(0, pooled + 1), pl.ds(0, members)], late_recv.at[0])
     lax.fori_loop(0, rows - 1, late_row, 0)
     final = (rows - 1 + REACH) % rows
     last_h[...] = held[pl.ds(latest * members, members), final]
     last_a[...] = got_a[rows - 1, pl.ds(0, members)]
-    take(got_b.at[rows - 1, pl.ds(0, members)], b_recv.at[rows - 1, 0])
+    take(got_b.at[rows - 1, pl.ds(0, members)], late_recv.at[rows - 1 - pooled])
     last_b[...] = got_b[rows - 1, pl.ds(0, members)]
     take(held.at[pl.ds(0, (L - 1) * members)], back_send.at[0])
 
@@ -427,7 +436,8 @@
             pltpu.VMEM((rows, ens, cols, head), bf16),
             pltpu.VMEM((rows, ens, cols, tail), bf16),
             pltpu.VMEM(fields.shape, bf16),
-            pltpu.SemaphoreType.REGULAR((2,)), pltpu.SemaphoreType.REGULAR((2,)), dma((1,)), dma((3, L - 1)), dma((2,)), dma((2, 2)), dma((2,)), dma((10,)), dma((1,)), dma((1,)), dma((rows, 2)),
+            pltpu.SemaphoreType.REGULAR((2,)), pltpu.SemaphoreType.REGULAR((2,)), dma((1,)), dma((2, L - 1)), dma((2,)), dma((2, 2)), dma((2,)), dma((10,)), dma((1,)), dma((1,)), dma((rows,) if rows % 2 else (rows // 2,)),
+            dma((rows - max(rows // 2 - 1, 0),)), dma((1,)),
         ],
         compiler_params=pltpu.CompilerParams(
             collective_id=0, has_side_effects=True, vmem_limit_bytes=48 * 2**20),

time: 118 us -> 118 us (level)
  no operation moved by 1% of the time
where the time goes in v6:
time: 118 us; the launch traced here: 116 us
  Pallas kernels  116 us (98%)
    pallas_call x1, Pallas kernels, block(): pl.pallas_call(functools.partial(block_kernel, L, T, members), out_shape=...  114 us

profile of v6, /device:TPU:0, one launch (start us, length us, event | category | flops | bytes accessed | tf_op | source)
XLA Modules:
  0.0 116.2 jit_solution(17441647850042796852)
XLA Ops:
  0.0 114.4 %block.1 = (bf16[4,8,64,640]{3,2,1,0:T(8,128)(2,1)S(1)}, bf16[1,64,128]{2,1,0:T(8,128)(2,1)S(1)}, bf16[1,64,512]{2,1,0:T(8,128)(2,1)S(1)}, bf16[1,64,640]{2,1,0:...) custom-call(bf16[4,8,64,640]{3,2,1,0:T(8,128)(2,1)} %fields.1, ...), custom_call_target="tpu_custom_call" | custom-call | tf_op jit(solution)/shard_map/block/pallas_call | solution.py:420
  114.5 1.7 %last.1 = bf16[4,8,64,640]{3,2,1,0:T(8,128)(2,1)} custom-call(bf16[4,8,64,640]{3,2,1,0:T(8,128)(2,1)S(1)} %get-tuple-element.13.done, bf16[1,64,128]{2,1,0:T(8,128)(2,1)S(1)} %get-tuple-element.14.last_a, bf16[1,64,512]{2,1,0:T(8,128)(2,1)S(1)} %get-tuple-element.15.last_b, bf16[1,64,640]{2,1,0:T(8,128)(2,1)S(1)} %get-tuple-element.16.last_h, ...), custom_call_target="tpu_custom_call" | custom-call | tf_op jit(solution)/shard_map/last/pallas_call | solution.py:447
